TPU v7x, 32 devices: a whole 2x2x4 slice. The times are simulated.
32 devices in a mesh: grp: 4 (over y, x), dev: 8 (over z, core).
Axes of the slice: x: 2, y: 2, z: 4, core: 2. Of those that a mesh axis runs over, the one named last changes fastest.
Arguments:
- q_lat: bfloat16 [128, 64, 576], P(('grp', 'dev')), parts along dimension 0, may hold values from -40 to 40
- latent_cache: bfloat16 [128, 256, 576], P(('grp', 'dev')), parts along dimension 0, may hold values from -8 to 8
- lengths: int32 [128], P('grp'), parts along dimension 0, may hold values from 32 to 256, as said below
- moves: int32 [64, 3], P('grp'), parts along dimension 0, may hold values from 0 to 31, as said below
- hidden_in: bfloat16 [128, 3584], P(('grp', 'dev')), parts along dimension 0, may hold values from -6 to 6
- norm_gain: bfloat16 [3584], replicated, may hold values from 0.25 to 1.75
- w_up: bfloat16 [3584, 10240], P(None, 'dev'), may hold values from -0.09375 to 0.09375
- w_down: bfloat16 [10240, 3584], P('dev'), may hold values from -0.0625 to 0.0625
- queue_counts: int32 [32, 8], P(('grp', 'dev')), parts along dimension 0, may hold values from 0 to 63
- deadline: int32 [128], P(('grp', 'dev')), parts along dimension 0, may hold values from 0 to 7
Outputs:
- attn_out: bfloat16 [128, 64, 512], P(('grp', 'dev')), parts along dimension 0
- new_cache: bfloat16 [128, 256, 576], P(('grp', 'dev')), parts along dimension 0
- mixed: bfloat16 [128, 3584], P(('grp', 'dev')), parts along dimension 0
- bucket_load: float32 [32], P('grp'), parts along dimension 0
There are 4 independent parts, one for each index of `grp`. A program takes and returns all parts, laid end to end along the dimension named above; an argument that names none is the same for every part. Nothing has to cross between parts.
Inputs may be any that keep to these rules, and one draw needn't show every extreme that they name: `lengths`: every length is at least 32; some request has exactly 256. `moves`: entry j * 8 + s (j below 2) has source device s and names a request of device s (requests r lie on device r // 4); the requests listed for one device are distinct. In round j every source s sends to (s + k_j) mod 8, with k_j between 1 and 7 the same for all sources of the round and different between rounds; one of the rounds has k_j = 4.
All inputs are finite; a program needn't handle non-finite values.
Results may differ from a plain program's by a relative error of at most 0.002.
The roundings to bfloat16 on the way count: a program that leaves them out, or rounds other values in their place, can miss the bound.
Values may be sent and summed in bfloat16 or wider, within the bound.
A program may use at most 128 MiB of HBM per device.

v0:
```python
from functools import partial
import jax
import jax.numpy as jnp
from jax import lax
from jax.sharding import PartitionSpec as P

VL = 512
MOVE_DEV = 2
BUCKETS = 8
softmax_scale = 192.0 ** (-0.5)


def for_sending(x):

    def short(part):
        return part.astype(jnp.bfloat16) if part.dtype == jnp.float32 else part

    return jax.tree.map(short, x)


def shifted(value, axis, steps):
    count = lax.axis_size(axis)
    pairs = [(source, (source + steps) % count) for source in range(count)]
    return lax.ppermute(value, axis, pairs)


def attend(queries, latent, context_lengths):
    row_count = queries.shape[0]
    head_count = queries.shape[1]
    block_size = min(128, latent.shape[1])
    block_count = (jnp.max(context_lengths) + block_size - 1) // block_size
    initial = (
        jnp.full((row_count, head_count), -1e30, jnp.float32),
        jnp.zeros((row_count, head_count), jnp.float32),
        jnp.zeros((row_count, head_count, VL), jnp.float32),
    )

    def advance(block_index, carried):
        running_max, running_sum, accumulated = carried
        key_block = lax.dynamic_slice_in_dim(latent, block_index * block_size, block_size, 1)
        scores = (
            jnp.einsum("rhc,rkc->rhk", queries, key_block, preferred_element_type=jnp.float32)
            * softmax_scale
        )
        positions = block_index * block_size + jnp.arange(block_size, dtype=jnp.int32)
        included = positions[None, None, :] < context_lengths[:, None, None]
        scores = jnp.where(included, scores, jnp.float32(-1e30))
        new_max = jnp.maximum(running_max, jnp.max(scores, axis=-1))
        factor = jnp.exp(running_max - new_max)
        weights = jnp.where(included, jnp.exp(scores - new_max[:, :, None]), jnp.float32(0.0))
        running_sum = running_sum * factor + jnp.sum(weights, axis=-1)
        product = jnp.einsum(
            "rhk,rkc->rhc",
            weights.astype(jnp.bfloat16),
            key_block[:, :, :VL],
            preferred_element_type=jnp.float32,
        )
        accumulated = accumulated * factor[:, :, None] + product
        return (new_max, running_sum, accumulated)

    final_max, final_sum, accumulated = lax.fori_loop(0, block_count, advance, initial)
    return (accumulated / final_sum[:, :, None]).astype(jnp.bfloat16)


def moved_by(offset, single_row):
    return jax.tree.map(
        lambda part, own: part.astype(own.dtype),
        shifted(for_sending(single_row), "dev", offset),
        single_row,
    )


def send_round(single_row, round_distance, devices):
    branches = [partial(moved_by, offset) for offset in range(1, devices)]
    return lax.switch(round_distance - 1, branches, single_row)


def per_device(
    q_lat, latent_cache, lengths, moves, hidden_in, norm_gain, w_up, w_down, queue_counts, deadline
):
    devices = lax.axis_size("dev")
    my_index = lax.axis_index("dev")
    row_count = latent_cache.shape[0]
    context = latent_cache.shape[1]
    rounds = moves.reshape(MOVE_DEV, devices, 3)
    own_moves = rounds[:, my_index, :]
    leaving = own_moves[:, 0] - my_index * row_count
    distance = (own_moves[:, 2] - my_index) % devices
    own_lengths = lax.dynamic_slice_in_dim(lengths, my_index * row_count, row_count)
    payload = latent_cache[leaving]
    arrivals = []
    for round_index in range(MOVE_DEV):
        arrivals.append(send_round(payload[round_index], distance[round_index], devices))
    travelled = jnp.stack(arrivals, axis=0)
    new_cache = latent_cache.at[leaving].set(travelled[:, :context])
    attn_out = attend(q_lat, latent_cache, own_lengths)
    widened = hidden_in.astype(jnp.float32)
    scaled = lax.rsqrt(jnp.mean(widened * widened, axis=-1, keepdims=True) + 1e-06)
    normed = (widened * scaled * norm_gain.astype(jnp.float32)[None, :]).astype(jnp.bfloat16)
    running = (deadline[:, None] == jnp.arange(BUCKETS, dtype=jnp.int32)[None, :]).astype(
        jnp.float32
    )
    bucket_terms = queue_counts.astype(jnp.float32)[0] + jnp.sum(running, axis=0)
    all_rows = lax.all_gather(normed, "dev", axis=0, tiled=True)
    bucket_load = lax.psum(bucket_terms, "dev")
    hidden_units = jax.nn.silu(jnp.dot(all_rows, w_up, preferred_element_type=jnp.float32)).astype(
        jnp.bfloat16
    )
    partial_sum = lax.psum_scatter(
        jnp.dot(hidden_units, w_down, preferred_element_type=jnp.float32),
        "dev",
        scatter_dimension=0,
        tiled=True,
    )
    mixed = (widened + partial_sum).astype(jnp.bfloat16)
    return (attn_out, new_cache, mixed, bucket_load)


def solution(mesh):
    return jax.shard_map(
        per_device,
        mesh=mesh,
        in_specs=(
            P(("grp", "dev"), None, None),
            P(("grp", "dev"), None, None),
            P("grp"),
            P("grp", None),
            P(("grp", "dev"), None),
            P(),
            P(None, "dev"),
            P("dev", None),
            P(("grp", "dev"), None),
            P(("grp", "dev")),
        ),
        out_specs=(
            P(("grp", "dev"), None, None),
            P(("grp", "dev"), None, None),
            P(("grp", "dev"), None),
            P("grp"),
        ),
        check_vma=False,
    )
```

profile of v0, /device:TPU:0, one launch (start us, length us, event | category | flops | bytes accessed | tf_op | source)
XLA Modules:
  0.0 112.7 jit_solution(7425908061489002161)
XLA Ops:
  7.2 0.6 copy-done.4
  8.2 16.0 %all-gather = bf16[8,4,3584]{2,1,0:T(4,128)(2,1)S(1)} all-gather(bf16[1,4,3584]{2,1,0:T(4,128)(2,1)S(1)} %fusion.19), channel_id=1, replica_groups=mesh['grp'=4,'dev'=8] {'dev'}, dimensions={0}, use_global_device_ids=true | all-gather | bytes 258048 | tf_op jit(solution)/shard_map/all_gather | solution.py:104
  24.2 10.4 %fusion.13 = f32[32,3584]{1,0:T(8,128)} fusion(bf16[1280,3584]{1,0:T(8,128)(2,1)} %param.33, bf16[32,3584]{1,0:T(8,128)(2,1)S(1)} %reshape.87, bf16[3584,1280]{1,0:T(8,128)(2,1)} %param.32), kind=kOutput, calls=%fused_computation.41 | convolution fusion | flops 587407360 | bytes 19038208 | tf_op jit(solution)/shard_map/dot_general | solution.py:110
  34.7 0.7 fusion.23
  36.2 1.0 while.14
  36.3 0.3 fusion.40
  36.7 0.2 fusion.41
  36.9 0.4 convolution_add_fusion.2
  37.7 0.6 fusion.25
  38.3 0.6 gather_fusion
  38.9 0.3 copy.53
  40.5 16.7 %conditional.3 = (bf16[1,256,576]{2,1,0:T(8,128)(2,1)}) conditional(s32[]{:T(128)} %bitcast.31, bf16[2,256,576]{2,1,0:T(8,128)(2,1)S(1)} %copy.53, bf16[2,256,576]{2,1,0:T(8,128)(2,1)S(1)} %copy.53, bf16[2,256,576]{2,1,0:T(8,128)(2,1)S(1)} %copy.53, bf16[2,256,576]{2,1,0:T(8,128)(2,1)S(1)} %copy.53, ...), branch_computations={%region_12.13_spmd, %region_13.14_spmd, %region_14.15_spmd, %regio... | conditional | bytes 1769520 | solution.py:75
  40.6 2.5 %collective-permute-start.9 = (bf16[256,576]{1,0:T(8,128)(2,1)S(1)}, bf16[256,576]{1,0:T(8,128)(2,1)}, u32[]{:S(2)}, u32[]{:S(2)}) collective-permute-start(bf16[256,576]{1,0:T(8,128)(2,1)S(1)} %slice_bitcast_fusion.9), channel_id=1, source_target_pairs={{0,3},{1,4},{2,5},{3,6},{4,7},{5,0},{6,1},{7,2},{8,11},{9,12},{10,... | collective-permute-start | bytes 884744 | tf_op jit(solution)/shard_map/cond/branch_2_fun/ppermute | solution.py:24
  43.1 14.1 %collective-permute-done.9 = bf16[256,576]{1,0:T(8,128)(2,1)} collective-permute-done((bf16[256,576]{1,0:T(8,128)(2,1)S(1)}, bf16[256,576]{1,0:T(8,128)(2,1)}, u32[]{:S(2)}, u32[]{:S(2)}) %collective-permute-start.9) | collective-permute-done | bytes 294944 | tf_op jit(solution)/shard_map/cond/branch_2_fun/ppermute | solution.py:24
  57.2 16.8 %conditional.2 = (bf16[1,256,576]{2,1,0:T(8,128)(2,1)}) conditional(s32[]{:T(128)} %bitcast.30, bf16[2,256,576]{2,1,0:T(8,128)(2,1)S(1)} %copy.53, bf16[2,256,576]{2,1,0:T(8,128)(2,1)S(1)} %copy.53, bf16[2,256,576]{2,1,0:T(8,128)(2,1)S(1)} %copy.53, bf16[2,256,576]{2,1,0:T(8,128)(2,1)S(1)} %copy.53, ...), branch_computations={%region_5.6_spmd, %region_6.7_spmd, %region_7.8_spmd, %region_8.9_... | conditional | bytes 1769520 | solution.py:75
  57.4 16.7 %collective-permute-done.3 = bf16[256,576]{1,0:T(8,128)(2,1)} collective-permute-done((bf16[256,576]{1,0:T(8,128)(2,1)S(1)}, bf16[256,576]{1,0:T(8,128)(2,1)}, u32[]{:S(2)}, u32[]{:S(2)}) %collective-permute-start.3) | collective-permute-done | bytes 294944 | tf_op jit(solution)/shard_map/cond/branch_3_fun/ppermute | solution.py:24
  74.2 1.2 %pad_maximum_fusion = bf16[2,256,576]{2,1,0:T(8,128)(2,1)S(1)} fusion(bf16[1,256,576]{2,1,0:T(8,128)(2,1)} %get-tuple-element.231, bf16[1,256,576]{2,1,0:T(8,128)(2,1)} %get-tuple-element.230), kind=kLoop, calls=%fused_computation.35 | loop fusion | flops 294912 | bytes 1179648 | tf_op jit(solution)/shard_map/stack | solution.py:94
  75.4 0.2 copy.67
  75.6 14.2 %psum.7 = f32[8]{0:T(128)} all-reduce(f32[8]{0:T(128)S(1)} %bitcast_add_fusion), channel_id=1, replica_groups=mesh['grp'=4,'dev'=8] {'dev'}, use_global_device_ids=true, to_apply=%region_23.24 | all-reduce | flops 8 | bytes 64 | tf_op jit(solution)/shard_map/psum | solution.py:105
  89.8 0.8 scatter_fusion
  90.6 0.7 dynamic-slice
  92.0 0.8 divide_convert_fusion
  92.8 11.5 %all-reduce.3.cloned.1.call-done = f32[32,3584]{1,0:T(8,128)} async-done(((f32[32,3584]{1,0:T(8,128)}), f32[32,3584]{1,0:T(8,128)}) %all-reduce.3.cloned.1.call-update) | async-done | bytes 458768
  104.3 1.5 %fusion.18 = bf16[4,3584]{1,0:T(4,128)(2,1)} fusion(bf16[4,3584]{1,0:T(4,128)(2,1)S(1)} %copy-done.3, f32[32,3584]{1,0:T(8,128)} %all-reduce.3.cloned.1.call-done, u32[]{:T(128)S(6)} %multiply.7), kind=kLoop, calls=%fused_computation.46 | loop fusion | flops 43008 | bytes 114692 | tf_op jit(solution)/shard_map/convert_element_type | solution.py:115
  (45 shorter events, 1.3 us)
Async XLA Ops:
  7.2 0.7 copy-start.3
  7.2 0.7 copy-start.4
  7.2 97.2 %all-reduce.3.cloned.1.call-start = ((), (), s32[]{:S(2)}) async-start(), calls=%async_computation | async-start | bytes 917504
  24.2 10.5 %copy-start.6 = (s32[32]{0:T(128)S(1)}, s32[32]{0:T(128)}, u32[]{:S(2)}) copy-start(s32[32]{0:T(128)} %param.28) | copy-start | bytes 388
  24.2 12.0 %copy-start.1 = (bf16[4,256,576]{1,2,0:T(8,128)(2,1)S(1)}, bf16[4,256,576]{1,2,0:T(8,128)(2,1)}, u32[]{:S(2)}) copy-start(bf16[4,256,576]{1,2,0:T(8,128)(2,1)} %param.27) | copy-start | bytes 3538948
  24.2 12.0 %copy-start.2 = (bf16[4,64,576]{2,1,0:T(8,128)(2,1)S(1)}, bf16[4,64,576]{2,1,0:T(8,128)(2,1)}, u32[]{:S(2)}) copy-start(bf16[4,64,576]{2,1,0:T(8,128)(2,1)} %param.26) | copy-start | bytes 884740
  36.2 1.1 copy-start.5
  40.6 16.7 %collective-permute-start.9 = (bf16[256,576]{1,0:T(8,128)(2,1)S(1)}, bf16[256,576]{1,0:T(8,128)(2,1)}, u32[]{:S(2)}, u32[]{:S(2)}) collective-permute-start(bf16[256,576]{1,0:T(8,128)(2,1)S(1)} %slice_bitcast_fusion.9), channel_id=1, source_target_pairs={{0,3},{1,4},{2,5},{3,6},{4,7},{5,0},{6,1},{7,2},{8,11},{9,12},{10,... | collective-permute-start | bytes 884744 | tf_op jit(solution)/shard_map/cond/branch_2_fun/ppermute | solution.py:24
  57.2 16.8 %copy-start.7 = (s32[4]{0:T(128)S(1)}, s32[4]{0:T(128)}, u32[]{:S(2)}) copy-start(s32[4]{0:T(128)} %param.35) | copy-start | bytes 52
  57.3 16.8 %collective-permute-start.3 = (bf16[256,576]{1,0:T(8,128)(2,1)S(1)}, bf16[256,576]{1,0:T(8,128)(2,1)}, u32[]{:S(2)}, u32[]{:S(2)}) collective-permute-start(bf16[256,576]{1,0:T(8,128)(2,1)S(1)} %slice_bitcast_fusion.3), channel_id=1, source_target_pairs={{0,4},{1,5},{2,6},{3,7},{4,0},{5,1},{6,2},{7,3},{8,12},{9,13},{10,... | collective-permute-start | bytes 884744 | tf_op jit(solution)/shard_map/cond/branch_3_fun/ppermute | solution.py:24
  74.1 1.3 %copy-start.8 = (s32[1,8]{1,0:T(1,128)S(1)}, s32[1,8]{1,0:T(1,128)}, u32[]{:S(2)}) copy-start(s32[1,8]{1,0:T(1,128)} %param.34) | copy-start | bytes 100
  75.6 15.0 %copy-start.9 = (u32[32]{0:T(128)S(1)}, u32[32]{0:T(128)}, u32[]{:S(2)}) copy-start(u32[32]{0:T(128)} %constant.94) | copy-start | bytes 388
  90.6 15.3 %copy-start = (bf16[4,256,576]{1,2,0:T(8,128)(2,1)}, bf16[4,256,576]{1,2,0:T(8,128)(2,1)S(1)}, u32[]{:S(2)}) copy-start(bf16[4,256,576]{1,2,0:T(8,128)(2,1)S(1)} %scatter_fusion) | copy-start | bytes 3538948
Sparse Core Ops, SparseCore 0:
  34.8 69.4 all-reduce.2
where the time goes:
time: 113 us
  waiting for transfers between devices  42.4 us (38%)
  blocking collectives  30.2 us (27%)
  between operations  16.9 us (15%)
  matrix products  11.1 us (10%)
  other arithmetic  5.04 us (4%)
  local copies, waits for them, and re-layouts  4.32 us (4%)
  starting transfers between devices  2.65 us (2%)
    ppermute x2, waiting for transfers between devices, shifted(): return lax.ppermute(value, axis, pairs)  30.8 us
    all_gather x1, blocking collectives, per_device(): all_rows = lax.all_gather(normed, 'dev', axis=0, tiled=True)  16 us
    psum x1, blocking collectives, per_device(): bucket_load = lax.psum(bucket_terms, 'dev')  14.2 us
    unnamed x2, waiting for transfers between devices  11.6 us
    dot_general x1, matrix products, per_device(): jnp.dot(hidden_units, w_down, preferred_element_type=jnp.float32)  10.4 us
    ppermute x2, starting transfers between devices, shifted(): return lax.ppermute(value, axis, pairs)  2.61 us
  transfers between devices with their start and end apart: 3, of which 3 were waited for; matrix products, arithmetic and copies ran while one was open for 7% of the time, Pallas kernels for 0%

commit v1 on v0

--- a/solution.py
+++ b/solution.py
@@ -101,7 +101,12 @@
         jnp.float32
     )
     bucket_terms = queue_counts.astype(jnp.float32)[0] + jnp.sum(running, axis=0)
-    all_rows = lax.all_gather(normed, "dev", axis=0, tiled=True)
+    ring = [normed]
+    for hop in range(7):
+        ring.append(lax.ppermute(ring[-1], "dev", [(dev, (dev + 1) % 8) for dev in range(8)]))
+    all_rows = jnp.roll(
+        jnp.concatenate(ring[::-1], axis=0), (lax.axis_index("dev") + 1) * ring[0].shape[0], axis=0
+    )
     bucket_load = lax.psum(bucket_terms, "dev")
     hidden_units = jax.nn.silu(jnp.dot(all_rows, w_up, preferred_element_type=jnp.float32)).astype(
         jnp.bfloat16

time: 113 us -> 159 us (1.41)
  waiting for transfers between devices: 42.4 us -> 103 us
  blocking collectives: 30.2 us -> 17.6 us
  starting transfers between devices: 2.65 us -> 0.73 us
    unnamed x2, waiting for transfers between devices: 11.6 us -> 53.4 us
    ppermute x0 -> x7, waiting for transfers between devices: none -> 22.2 us  [per_device(): lax.ppermute(ring[-1], 'dev', [(dev, (dev + 1) % 8) for dev in range(8)])]
    all_gather x1 -> x0, blocking collectives: 16 us -> none  [per_device(): all_rows = lax.all_gather(normed, 'dev', axis=0, tiled=True)]
    ppermute x2, waiting for transfers between devices: 30.8 us -> 26.8 us  [shifted(): return lax.ppermute(value, axis, pairs)]
    psum x1, blocking collectives: 14.2 us -> 17.6 us  [per_device(): bucket_load = lax.psum(bucket_terms, 'dev')]
    ppermute x2, starting transfers between devices: 2.61 us -> 0.13 us  [shifted(): return lax.ppermute(value, axis, pairs)]
  transfers between devices with their start and end apart: 3 -> 10, of which waited for: 3 -> 8; matrix products, arithmetic and copies ran while one was open for 7% -> 5% of each run, Pallas kernels for 0% -> 0%
where the time goes in v1:
time: 159 us
  waiting for transfers between devices  103 us (65%)
  blocking collectives  17.6 us (11%)
  between operations  16.9 us (11%)
  matrix products  11 us (7%)
  other arithmetic  5.03 us (3%)
  local copies, waits for them, and re-layouts  4.73 us (3%)
    unnamed x2, waiting for transfers between devices  53.4 us
    ppermute x2, waiting for transfers between devices, shifted(): return lax.ppermute(value, axis, pairs)  26.8 us
    ppermute x7, waiting for transfers between devices, per_device(): lax.ppermute(ring[-1], 'dev', [(dev, (dev + 1) % 8) for dev in range(8)])  22.2 us
    psum x1, blocking collectives, per_device(): bucket_load = lax.psum(bucket_terms, 'dev')  17.6 us
    dot_general x1, matrix products, per_device(): jnp.dot(hidden_units, w_down, preferred_element_type=jnp.float32)  10.3 us
  transfers between devices with their start and end apart: 10, of which 8 were waited for; matrix products, arithmetic and copies ran while one was open for 5% of the time, Pallas kernels for 0%

profile of v1, /device:TPU:0, one launch (start us, length us, event | category | flops | bytes accessed | tf_op | source)
XLA Modules:
  0.0 158.6 jit_solution(8248070877447756012)
XLA Ops:
  7.3 0.8 copy-done.4
  8.3 0.5 collective-permute-start.14
  8.9 0.7 fusion.30
  10.4 1.0 while.14
  11.0 0.4 convolution_add_fusion.2
  11.6 2.8 %collective-permute-done.14 = bf16[4,3584]{1,0:T(4,128)(2,1)S(1)} collective-permute-done((bf16[4,3584]{1,0:T(4,128)(2,1)S(1)}, bf16[4,3584]{1,0:T(4,128)(2,1)S(1)}, u32[]{:S(2)}, u32[]{:S(2)}) %collective-permute-start.14) | collective-permute-done | bytes 28704 | tf_op jit(solution)/shard_map/ppermute | solution.py:106
  14.6 4.9 %collective-permute-done.15 = bf16[4,3584]{1,0:T(4,128)(2,1)S(1)} collective-permute-done((bf16[4,3584]{1,0:T(4,128)(2,1)S(1)}, bf16[4,3584]{1,0:T(4,128)(2,1)S(1)}, u32[]{:S(2)}, u32[]{:S(2)}) %collective-permute-start.15) | collective-permute-done | bytes 28704 | tf_op jit(solution)/shard_map/ppermute | solution.py:106
  19.7 4.9 %collective-permute-done.16 = bf16[4,3584]{1,0:T(4,128)(2,1)S(1)} collective-permute-done((bf16[4,3584]{1,0:T(4,128)(2,1)S(1)}, bf16[4,3584]{1,0:T(4,128)(2,1)S(1)}, u32[]{:S(2)}, u32[]{:S(2)}) %collective-permute-start.16) | collective-permute-done | bytes 28704 | tf_op jit(solution)/shard_map/ppermute | solution.py:106
  24.6 5.1 %collective-permute-done.17 = bf16[4,3584]{1,0:T(4,128)(2,1)S(1)} collective-permute-done((bf16[4,3584]{1,0:T(4,128)(2,1)S(1)}, bf16[4,3584]{1,0:T(4,128)(2,1)S(1)}, u32[]{:S(2)}, u32[]{:S(2)}) %collective-permute-start.17) | collective-permute-done | bytes 28704 | tf_op jit(solution)/shard_map/ppermute | solution.py:106
  29.7 0.6 fusion.32
  30.3 4.5 %collective-permute-done.18 = bf16[4,3584]{1,0:T(4,128)(2,1)S(1)} collective-permute-done((bf16[4,3584]{1,0:T(4,128)(2,1)S(1)}, bf16[4,3584]{1,0:T(4,128)(2,1)S(1)}, u32[]{:S(2)}, u32[]{:S(2)}) %collective-permute-start.18) | collective-permute-done | bytes 28704 | tf_op jit(solution)/shard_map/ppermute | solution.py:106
  34.8 0.6 gather_fusion
  37.0 12.4 %conditional.3 = (bf16[1,256,576]{2,1,0:T(8,128)(2,1)}) conditional(s32[]{:T(128)} %bitcast.31, bf16[2,256,576]{2,1,0:T(8,128)(2,1)S(1)} %copy.53, bf16[2,256,576]{2,1,0:T(8,128)(2,1)S(1)} %copy.53, bf16[2,256,576]{2,1,0:T(8,128)(2,1)S(1)} %copy.53, bf16[2,256,576]{2,1,0:T(8,128)(2,1)S(1)} %copy.53, ...), branch_computations={%region_12.13_spmd, %region_13.14_spmd, %region_14.15_spmd, %regio... | conditional | bytes 1769520 | solution.py:75
  37.2 12.3 %collective-permute-done.9 = bf16[256,576]{1,0:T(8,128)(2,1)} collective-permute-done((bf16[256,576]{1,0:T(8,128)(2,1)S(1)}, bf16[256,576]{1,0:T(8,128)(2,1)}, u32[]{:S(2)}, u32[]{:S(2)}) %collective-permute-start.9) | collective-permute-done | bytes 294944 | tf_op jit(solution)/shard_map/cond/branch_2_fun/ppermute | solution.py:24
  49.5 14.7 %conditional.2 = (bf16[1,256,576]{2,1,0:T(8,128)(2,1)}) conditional(s32[]{:T(128)} %bitcast.30, bf16[2,256,576]{2,1,0:T(8,128)(2,1)S(1)} %copy.53, bf16[2,256,576]{2,1,0:T(8,128)(2,1)S(1)} %copy.53, bf16[2,256,576]{2,1,0:T(8,128)(2,1)S(1)} %copy.53, bf16[2,256,576]{2,1,0:T(8,128)(2,1)S(1)} %copy.53, ...), branch_computations={%region_5.6_spmd, %region_6.7_spmd, %region_7.8_spmd, %region_8.9_... | conditional | bytes 1769520 | solution.py:75
  49.6 14.5 %collective-permute-done.3 = bf16[256,576]{1,0:T(8,128)(2,1)} collective-permute-done((bf16[256,576]{1,0:T(8,128)(2,1)S(1)}, bf16[256,576]{1,0:T(8,128)(2,1)}, u32[]{:S(2)}, u32[]{:S(2)}) %collective-permute-start.3) | collective-permute-done | bytes 294944 | tf_op jit(solution)/shard_map/cond/branch_3_fun/ppermute | solution.py:24
  64.1 1.2 pad_maximum_fusion
  65.3 17.6 %psum.7 = f32[8]{0:T(128)} all-reduce(f32[8]{0:T(128)S(1)} %bitcast_add_fusion), channel_id=1, replica_groups=mesh['grp'=4,'dev'=8] {'dev'}, use_global_device_ids=true, to_apply=%region_23.24 | all-reduce | flops 8 | bytes 64 | tf_op jit(solution)/shard_map/psum | solution.py:110
  83.2 0.8 scatter_fusion
  84.0 0.7 dynamic-slice
  85.7 10.3 %fusion.18 = f32[32,3584]{1,0:T(8,128)} fusion(bf16[1280,3584]{1,0:T(8,128)(2,1)} %param.33, bf16[3584,1280]{1,0:T(8,128)(2,1)} %param.32, bf16[64,3584]{1,0:T(8,128)(2,1)S(1)} %concatenate.6, s32[]{:T(128)S(6)} %select_n.53), kind=kOutput, calls=%fused_computation.40 | convolution fusion | flops 587407360 | bytes 19038212 | tf_op jit(solution)/shard_map/dot_general | solution.py:115
  96.0 0.8 divide_convert_fusion
  96.8 53.4 %all-reduce.3.cloned.1.call-done = f32[32,3584]{1,0:T(8,128)} async-done(((f32[32,3584]{1,0:T(8,128)}), f32[32,3584]{1,0:T(8,128)}) %all-reduce.3.cloned.1.call-update) | async-done | bytes 458768
  150.2 1.5 fusion.24
  (58 shorter events, 2.7 us)
Async XLA Ops:
  7.2 3.2 %copy-start.2 = (bf16[4,64,576]{2,1,0:T(8,128)(2,1)S(1)}, bf16[4,64,576]{2,1,0:T(8,128)(2,1)}, u32[]{:S(2)}) copy-start(bf16[4,64,576]{2,1,0:T(8,128)(2,1)} %param.26) | copy-start | bytes 884740
  7.2 3.2 %copy-start.1 = (bf16[4,256,576]{1,2,0:T(8,128)(2,1)S(1)}, bf16[4,256,576]{1,2,0:T(8,128)(2,1)}, u32[]{:S(2)}) copy-start(bf16[4,256,576]{1,2,0:T(8,128)(2,1)} %param.27) | copy-start | bytes 3538948
  7.2 1.7 %copy-start.6 = (s32[32]{0:T(128)S(1)}, s32[32]{0:T(128)}, u32[]{:S(2)}) copy-start(s32[32]{0:T(128)} %param.28) | copy-start | bytes 388
  7.2 0.9 copy-start.3
  7.2 0.8 copy-start.4
  7.2 143.0 %all-reduce.3.cloned.1.call-start = ((), (), s32[]{:S(2)}) async-start(), calls=%async_computation | async-start | bytes 917504
  8.3 6.1 %collective-permute-start.14 = (bf16[4,3584]{1,0:T(4,128)(2,1)S(1)}, bf16[4,3584]{1,0:T(4,128)(2,1)S(1)}, u32[]{:S(2)}, u32[]{:S(2)}) collective-permute-start(bf16[4,3584]{1,0:T(4,128)(2,1)S(1)} %fusion.23), channel_id=1, source_target_pairs={{0,1},{1,2},{2,3},{3,4},{4,5},{5,6},{6,7},{7,0},{8,9},{9,10},{10,1... | collective-permute-start | bytes 86024 | tf_op jit(solution)/shard_map/ppermute | solution.py:106
  10.3 1.1 copy-start.7
  10.3 1.2 copy-start.8
  10.4 1.2 copy-start.5
  14.4 5.1 %collective-permute-start.15 = (bf16[4,3584]{1,0:T(4,128)(2,1)S(1)}, bf16[4,3584]{1,0:T(4,128)(2,1)S(1)}, u32[]{:S(2)}, u32[]{:S(2)}) collective-permute-start(bf16[4,3584]{1,0:T(4,128)(2,1)S(1)} %collective-permute-done.14), channel_id=1, source_target_pairs={{0,1},{1,2},{2,3},{3,4},{4,5},{5,6},{6,7},{7,0},{8,9},{9,10},{10,1... | collective-permute-start | bytes 86024 | tf_op jit(solution)/shard_map/ppermute | solution.py:106
  19.5 5.1 %collective-permute-start.16 = (bf16[4,3584]{1,0:T(4,128)(2,1)S(1)}, bf16[4,3584]{1,0:T(4,128)(2,1)S(1)}, u32[]{:S(2)}, u32[]{:S(2)}) collective-permute-start(bf16[4,3584]{1,0:T(4,128)(2,1)S(1)} %collective-permute-done.15), channel_id=1, source_target_pairs={{0,1},{1,2},{2,3},{3,4},{4,5},{5,6},{6,7},{7,0},{8,9},{9,10},{10,1... | collective-permute-start | bytes 86024 | tf_op jit(solution)/shard_map/ppermute | solution.py:106
  24.6 5.1 %collective-permute-start.17 = (bf16[4,3584]{1,0:T(4,128)(2,1)S(1)}, bf16[4,3584]{1,0:T(4,128)(2,1)S(1)}, u32[]{:S(2)}, u32[]{:S(2)}) collective-permute-start(bf16[4,3584]{1,0:T(4,128)(2,1)S(1)} %collective-permute-done.16), channel_id=1, source_target_pairs={{0,1},{1,2},{2,3},{3,4},{4,5},{5,6},{6,7},{7,0},{8,9},{9,10},{10,1... | collective-permute-start | bytes 86024 | tf_op jit(solution)/shard_map/ppermute | solution.py:106
  29.7 5.1 %collective-permute-start.18 = (bf16[4,3584]{1,0:T(4,128)(2,1)S(1)}, bf16[4,3584]{1,0:T(4,128)(2,1)S(1)}, u32[]{:S(2)}, u32[]{:S(2)}) collective-permute-start(bf16[4,3584]{1,0:T(4,128)(2,1)S(1)} %collective-permute-done.17), channel_id=1, source_target_pairs={{0,1},{1,2},{2,3},{3,4},{4,5},{5,6},{6,7},{7,0},{8,9},{9,10},{10,1... | collective-permute-start | bytes 86024 | tf_op jit(solution)/shard_map/ppermute | solution.py:106
  34.8 29.3 %collective-permute-start.19 = (bf16[4,3584]{1,0:T(4,128)(2,1)S(1)}, bf16[4,3584]{1,0:T(4,128)(2,1)S(1)}, u32[]{:S(2)}, u32[]{:S(2)}) collective-permute-start(bf16[4,3584]{1,0:T(4,128)(2,1)S(1)} %collective-permute-done.18), channel_id=1, source_target_pairs={{0,1},{1,2},{2,3},{3,4},{4,5},{5,6},{6,7},{7,0},{8,9},{9,10},{10,1... | collective-permute-start | bytes 86024 | tf_op jit(solution)/shard_map/ppermute | solution.py:106
  37.1 12.4 %collective-permute-start.9 = (bf16[256,576]{1,0:T(8,128)(2,1)S(1)}, bf16[256,576]{1,0:T(8,128)(2,1)}, u32[]{:S(2)}, u32[]{:S(2)}) collective-permute-start(bf16[256,576]{1,0:T(8,128)(2,1)S(1)} %slice_bitcast_fusion.9), channel_id=1, source_target_pairs={{0,3},{1,4},{2,5},{3,6},{4,7},{5,0},{6,1},{7,2},{8,11},{9,12},{10,... | collective-permute-start | bytes 884744 | tf_op jit(solution)/shard_map/cond/branch_2_fun/ppermute | solution.py:24
  49.5 14.6 %collective-permute-start.3 = (bf16[256,576]{1,0:T(8,128)(2,1)S(1)}, bf16[256,576]{1,0:T(8,128)(2,1)}, u32[]{:S(2)}, u32[]{:S(2)}) collective-permute-start(bf16[256,576]{1,0:T(8,128)(2,1)S(1)} %slice_bitcast_fusion.3), channel_id=1, source_target_pairs={{0,4},{1,5},{2,6},{3,7},{4,0},{5,1},{6,2},{7,3},{8,12},{9,13},{10,... | collective-permute-start | bytes 884744 | tf_op jit(solution)/shard_map/cond/branch_3_fun/ppermute | solution.py:24
  64.1 21.2 %collective-permute-start.20 = (bf16[4,3584]{1,0:T(4,128)(2,1)S(1)}, bf16[4,3584]{1,0:T(4,128)(2,1)S(1)}, u32[]{:S(2)}, u32[]{:S(2)}) collective-permute-start(bf16[4,3584]{1,0:T(4,128)(2,1)S(1)} %collective-permute-done.19), channel_id=1, source_target_pairs={{0,1},{1,2},{2,3},{3,4},{4,5},{5,6},{6,7},{7,0},{8,9},{9,10},{10,1... | collective-permute-start | bytes 86024 | tf_op jit(solution)/shard_map/ppermute | solution.py:106
  83.2 0.8 copy-start.9
  84.0 12.0 %copy-start = (bf16[4,256,576]{1,2,0:T(8,128)(2,1)}, bf16[4,256,576]{1,2,0:T(8,128)(2,1)S(1)}, u32[]{:S(2)}) copy-start(bf16[4,256,576]{1,2,0:T(8,128)(2,1)S(1)} %scatter_fusion) | copy-start | bytes 3538948
Sparse Core Ops, SparseCore 0:
  96.1 54.0 all-reduce.2
